TPU v7x, 32 devices: a whole 2x2x4 slice. The times are simulated.
32 devices in a mesh: row: 4 (over y, x), col: 8 (over z, core).
Axes of the slice: x: 2, y: 2, z: 4, core: 2. Of those that a mesh axis runs over, the one named last changes fastest.
Arguments:
- gradient: float32 [6144, 12288], P(('row', 'col')), may hold values from -200 to 200
Outputs:
- preconditioned: float32 [6144, 12288], P(('row', 'col'))
All inputs are finite; a program needn't handle non-finite values.
Results may differ from a plain program's by a relative error of at most 0.00023.
Values sent between devices are 32-bit elements; how exact they have to be, the bound alone decides.
A program may use at most 128 MiB of HBM per device.

v0:
```python
import jax
import jax.numpy as jnp
from jax import lax
from jax.sharding import PartitionSpec as P

D = 12288
BLOCK = 768
ITERS = 2


def product(first, second):
    return jnp.matmul(first, second, precision=lax.Precision.HIGHEST)


def inverse_root(gram_matrix):
    matrix_order = gram_matrix.shape[-1]
    identity = jnp.eye(matrix_order, dtype=gram_matrix.dtype)
    norm_scale = jnp.sqrt(jnp.sum(gram_matrix * gram_matrix, axis=(-2, -1), keepdims=True)) + 1e-06
    iterate = gram_matrix / norm_scale
    root_now = identity
    for iteration in range(ITERS):
        factor = (5.0 * identity - iterate) * 0.25
        root_now = factor if iteration == 0 else product(root_now, factor)
        if iteration + 1 < ITERS:
            square = product(factor, factor)
            iterate = product(product(square, square), iterate)
    return root_now * norm_scale ** (-0.25)


def empty_root(gram_matrix):
    return jnp.zeros_like(gram_matrix)


def local(gradient):
    tile_grad = lax.all_to_all(gradient, "col", split_axis=1, concat_axis=0, tiled=True)
    row_blocks = tile_grad.shape[0] // BLOCK
    col_blocks = tile_grad.shape[1] // BLOCK
    blocks = tile_grad.reshape(row_blocks, BLOCK, col_blocks, BLOCK)
    left_part = jnp.einsum("aibj,akbj->aik", blocks, blocks, precision=lax.Precision.HIGHEST) / D
    right_part = jnp.einsum("aibj,aibk->bjk", blocks, blocks, precision=lax.Precision.HIGHEST) / D
    left_gram = lax.psum(left_part, "col")
    right_gram = lax.psum(right_part, "row")
    row_here = lax.axis_index("row")
    col_here = lax.axis_index("col")
    row_total = lax.axis_size("row")
    col_total = lax.axis_size("col")
    left_owners = []
    left_owned = []
    for block_row in range(row_blocks):
        owner_col = (row_here + 1 + block_row) % col_total
        left_owners.append(owner_col)
        left_owned.append(
            lax.cond(col_here == owner_col, inverse_root, empty_root, left_gram[block_row])
        )
    right_owners = []
    right_owned = []
    for block_col in range(col_blocks):
        owner_row = (col_here * col_blocks + block_col) % row_total
        right_owners.append(owner_row)
        right_owned.append(
            lax.cond(row_here == owner_row, inverse_root, empty_root, right_gram[block_col])
        )
    left_roots = lax.psum(jnp.stack(left_owned), "col")
    right_roots = lax.psum(jnp.stack(right_owned), "row")
    mixed_rows = jnp.einsum("aik,akbj->aibj", left_roots, blocks, precision=lax.Precision.HIGHEST)
    result = jnp.einsum("aibj,bjl->aibl", mixed_rows, right_roots, precision=lax.Precision.HIGHEST)
    tile_out = result.reshape(tile_grad.shape[0], tile_grad.shape[1])
    return lax.all_to_all(tile_out, "col", split_axis=0, concat_axis=1, tiled=True)


def solution(mesh):
    in_specs = (P(("row", "col"), None),)
    out_specs = P(("row", "col"), None)
    return jax.shard_map(local, mesh=mesh, in_specs=in_specs, out_specs=out_specs, check_vma=False)
```

profile of v0, /device:TPU:0, one launch (start us, length us, event | category | flops | bytes accessed | tf_op | source)
XLA Modules:
  0.0 988.0 jit_solution(14985175931717549455)
XLA Ops:
  6.5 0.0 all-reduce.9.cloned.1.call-start
  6.5 4.5 copy.45
  11.1 212.6 %all_to_all.35 = f32[192,8,1536]{2,0,1:T(8,128)} all-to-all(f32[192,8,1536]{2,0,1:T(8,128)S(1)} %bitcast.97), channel_id=1, replica_groups=mesh['row'=4,'col'=8] {'col'}, dimensions={1} | all-to-all | bytes 18874368 | tf_op jit(solution)/shard_map/all_to_all | solution.py:35
  223.7 12.1 %reshape.108 = f32[2,768,2,768]{3,2,1,0:T(2,128)} reshape(f32[8,192,1536]{2,1,0:T(8,128)} %bitcast.95) | data formatting | bytes 18874368 | tf_op jit(solution)/shard_map/reshape | solution.py:38
  235.7 29.4 %bitcast_multiply_fusion = f32[2,768,768]{2,1,0:T(8,128)} fusion(f32[2,768,2,768]{3,2,1,0:T(2,128)} %reshape.108), kind=kOutput, calls=%fused_computation.132 | convolution fusion | flops 21744451584 | bytes 14155776 | tf_op jit(solution)/shard_map/aibj,akbj->aik/dot_general | solution.py:39
  265.1 0.0 all-reduce.9.cloned.1.call-update
  265.1 0.6 all-reduce.5.cloned.1.call-start
  265.7 35.0 %bitcast_multiply_fusion.1 = f32[2,768,768]{2,1,0:T(8,128)} fusion(f32[2,768,2,768]{3,2,1,0:T(2,128)} %reshape.108), kind=kOutput, calls=%fused_computation.133 | convolution fusion | flops 21744451584 | bytes 14155776 | tf_op jit(solution)/shard_map/aibj,aibk->bjk/dot_general | solution.py:40
  300.7 0.0 all-reduce.5.cloned.1.call-update
  300.7 0.0 all-reduce.11.cloned.1.call-start
  300.8 69.8 %all-reduce.9.cloned.1.call-done = f32[2,768,768]{2,1,0:T(8,128)} async-done(((f32[2,768,768]{2,1,0:T(8,128)}), f32[2,768,768]{2,1,0:T(8,128)}) %all-reduce.9.cloned.1.call-update) | async-done | bytes 4718608 | tf_op jit(solution)/shard_map/psum | solution.py:41
  370.6 8.9 conditional.7
  370.6 0.2 stack.30
  379.5 14.3 %conditional.6 = (f32[1,768,768]{2,1,0:T(8,128)}) conditional(s32[]{:T(128)} %convert_element_type.18, () %tuple.39, f32[2,768,768]{2,1,0:T(8,128)} %all-reduce.9.cloned.1.call-done), branch_computations={%region_9.10_spmd, %region_10.0_spmd} | conditional | flops 21753888768 | bytes 44826712 | solution.py:53
  379.5 1.7 stack.28
  393.8 4.1 pad_maximum_fusion.1
  398.0 0.0 all-reduce.11.cloned.1.call-update
  398.0 0.0 all-reduce.7.cloned.1.call-start
  398.1 88.2 %all-reduce.5.cloned.1.call-done = f32[2,768,768]{2,1,0:T(8,128)} async-done(((f32[2,768,768]{2,1,0:T(8,128)}), f32[2,768,768]{2,1,0:T(8,128)}) %all-reduce.5.cloned.1.call-update) | async-done | bytes 4718608 | tf_op jit(solution)/shard_map/psum | solution.py:42
  486.2 9.1 conditional.5
  486.2 0.2 stack.26.clone
  495.3 39.0 %conditional.4 = (f32[1,768,768]{1,2,0:T(8,128)}) conditional(s32[]{:T(128)} %convert_element_type.16, () %tuple.37, f32[2,768,768]{2,1,0:T(8,128)} %all-reduce.5.cloned.1.call-done), branch_computations={%region_1.0_spmd, %region_2.4_spmd} | conditional | flops 21753888768 | bytes 49545304 | solution.py:61
  495.4 2.9 multiply_reduce_fusion
  499.0 8.7 fusion.5
  507.6 0.0 copy-start
  507.7 6.0 fusion.132
  513.6 0.0 copy-done
  513.6 7.4 fusion.7
  521.1 9.9 %multiply_bitcast_fusion = f32[1,768,768]{2,1,0:T(8,128)} fusion(f32[768,768]{1,0:T(8,128)} %fusion.7, f32[]{:T(128)S(6)} %pow.12, f32[2,768,768]{2,1,0:T(8,128)} %param.1, f32[]{:T(128)S(6)} %add.38), kind=kOutput, calls=%fused_computation.10 | convolution fusion | flops 5441716224 | bytes 7077896 | tf_op jit(solution)/shard_map/cond/branch_1_fun/dot_general | solution.py:12
  531.0 3.1 copy.29
  534.3 4.1 pad_maximum_fusion
  538.4 0.0 all-reduce.7.cloned.1.call-update
  538.4 56.6 %all-reduce.11.cloned.1.call-done = f32[2,768,768]{2,1,0:T(8,128)} async-done(((f32[2,768,768]{2,1,0:T(8,128)}), f32[2,768,768]{2,1,0:T(8,128)}) %all-reduce.11.cloned.1.call-update) | async-done | bytes 4718608 | tf_op jit(solution)/shard_map/psum | solution.py:63
  595.0 28.1 %fusion.118 = f32[2,768,2,768]{3,1,0,2:T(8,128)} fusion(f32[2,768,2,768]{3,2,1,0:T(2,128)} %reshape.108, f32[2,768,768]{2,1,0:T(8,128)} %all-reduce.11.cloned.1.call-done), kind=kOutput, calls=%fused_computation.123 | convolution fusion | flops 21743271936 | bytes 23592960 | tf_op jit(solution)/shard_map/aik,akbj->aibj/dot_general | solution.py:65
  623.1 87.4 %all-reduce.7.cloned.1.call-done = f32[2,768,768]{1,2,0:T(8,128)} async-done(((f32[2,768,768]{1,2,0:T(8,128)}), f32[2,768,768]{1,2,0:T(8,128)}) %all-reduce.7.cloned.1.call-update) | async-done | bytes 4718608 | tf_op jit(solution)/shard_map/psum | solution.py:64
  710.5 27.2 %fusion.125 = f32[2,768,2,768]{1,3,0,2:T(8,128)} fusion(f32[2,768,2,768]{3,1,0,2:T(8,128)} %fusion.118, f32[2,768,768]{1,2,0:T(8,128)} %all-reduce.7.cloned.1.call-done), kind=kOutput, calls=%fused_computation.134 | convolution fusion | flops 21743271936 | bytes 23592960 | tf_op jit(solution)/shard_map/aibj,bjl->aibl/dot_general | solution.py:66
  737.7 14.9 %copy.23 = f32[2,768,2,768]{3,2,1,0:T(2,128)} copy(f32[2,768,2,768]{1,3,0,2:T(8,128)} %fusion.125) | data formatting | bytes 18874368 | tf_op jit(solution)/shard_map/aibj,bjl->aibl/transpose | solution.py:66
  752.6 13.1 %all_to_all.29 = f32[8,192,1536]{2,1,0:T(8,128)} reshape(f32[2,768,2,768]{3,2,1,0:T(2,128)} %copy.23) | data formatting | bytes 18874368 | tf_op jit(solution)/shard_map/all_to_all | solution.py:68
  765.6 210.9 %all_to_all.36 = f32[8,192,1536]{2,1,0:T(8,128)S(1)} all-to-all(f32[8,192,1536]{2,1,0:T(8,128)} %all_to_all.29), channel_id=1, replica_groups=mesh['row'=4,'col'=8] {'col'}, dimensions={0} | all-to-all | bytes 18874368 | tf_op jit(solution)/shard_map/all_to_all | solution.py:68
  976.6 4.6 copy.33
Async XLA Ops:
  6.5 364.1 %all-reduce.9.cloned.1.call-start = ((), (), s32[]{:S(2)}) async-start(), calls=%async_computation.4 | async-start | bytes 9437184 | tf_op jit(solution)/shard_map/psum | solution.py:41
  265.1 221.1 %all-reduce.5.cloned.1.call-start = ((), (), s32[]{:S(2)}) async-start(), calls=%async_computation.2 | async-start | bytes 9437184 | tf_op jit(solution)/shard_map/psum | solution.py:42
  300.7 294.3 %all-reduce.11.cloned.1.call-start = ((), (), s32[]{:S(2)}) async-start(), calls=%async_computation.5 | async-start | bytes 9437184 | tf_op jit(solution)/shard_map/psum | solution.py:63
  398.0 312.5 %all-reduce.7.cloned.1.call-start = ((), (), s32[]{:S(2)}) async-start(), calls=%async_computation.3 | async-start | bytes 9437184 | tf_op jit(solution)/shard_map/psum | solution.py:64
  507.6 6.0 copy-start
Sparse Core Ops, SparseCore 0:
  265.3 105.2 all-reduce.8
  373.9 112.3 all-reduce.4
  488.6 106.3 all-reduce.10
  598.1 112.3 all-reduce.6
where the time goes:
time: 994 us; the launch traced here: 988 us
  blocking collectives  424 us (43%)
  waiting for transfers between devices  302 us (30%)
  matrix products  152 us (15%)
  local copies, waits for them, and re-layouts  54.1 us (5%)
  loops' own time  31.3 us (3%)
  between operations  13.5 us (1%)
  other arithmetic  11.2 us (1%)
    all_to_all x1, blocking collectives, local(): lax.all_to_all(gradient, 'col', split_axis=1, concat_axis=0, tiled=True)  213 us
    all_to_all x1, blocking collectives, local(): lax.all_to_all(tile_out, 'col', split_axis=0, concat_axis=1, tiled=True)  211 us
    psum x1, waiting for transfers between devices, local(): right_gram = lax.psum(right_part, 'row')  88.2 us
    psum x1, waiting for transfers between devices, local(): right_roots = lax.psum(jnp.stack(right_owned), 'row')  87.4 us
    psum x1, waiting for transfers between devices, local(): left_gram = lax.psum(left_part, 'col')  69.8 us
    psum x1, waiting for transfers between devices, local(): left_roots = lax.psum(jnp.stack(left_owned), 'col')  56.6 us
    dot_general x1, matrix products, local(): jnp.einsum('aibj,aibk->bjk', blocks, blocks, precision=lax.Precision.HIGH...  35 us
    dot_general x4, matrix products, product(): return jnp.matmul(first, second, precision=lax.Precision.HIGHEST)  32 us
  transfers between devices with their start and end apart: 4, of which 4 were waited for; matrix products, arithmetic and copies ran while one was open for 11% of the time, Pallas kernels for 0%

commit v1 on v0

--- a/solution.py
+++ b/solution.py
@@ -38,7 +38,11 @@
     blocks = tile_grad.reshape(row_blocks, BLOCK, col_blocks, BLOCK)
     left_part = jnp.einsum("aibj,akbj->aik", blocks, blocks, precision=lax.Precision.HIGHEST) / D
     right_part = jnp.einsum("aibj,aibk->bjk", blocks, blocks, precision=lax.Precision.HIGHEST) / D
-    left_gram = lax.psum(left_part, "col")
+    left_gram = left_part
+    for hop in (1, 2, 4):
+        left_gram = left_gram + lax.ppermute(
+            left_gram, "col", [(dev, dev ^ hop) for dev in range(8)]
+        )
     right_gram = lax.psum(right_part, "row")
     row_here = lax.axis_index("row")
     col_here = lax.axis_index("col")

time: 994 us -> 1150 us (1.16)
  waiting for transfers between devices: 302 us -> 447 us
    ppermute x0 -> x3, waiting for transfers between devices: none -> 276 us  [local(): lax.ppermute(left_gram, 'col', [(dev, dev ^ hop) for dev in range(8)])]
    psum x1, waiting for transfers between devices: 88.2 us -> 0.02 us  [local(): right_gram = lax.psum(right_part, 'row')]
    psum x1 -> x0, waiting for transfers between devices: 69.8 us -> none  [local(): left_gram = lax.psum(left_part, 'col')]
    psum x1, waiting for transfers between devices: 56.6 us -> 84.1 us  [local(): left_roots = lax.psum(jnp.stack(left_owned), 'col')]
  transfers between devices with their start and end apart: 4 -> 6, of which waited for: 4 -> 5; matrix products, arithmetic and copies ran while one was open for 11% -> 11% of each run, Pallas kernels for 0% -> 0%
where the time goes in v1:
time: 1150 us; the launch traced here: 1140 us
  waiting for transfers between devices  447 us (39%)
  blocking collectives  424 us (37%)
  matrix products  157 us (14%)
  local copies, waits for them, and re-layouts  54.1 us (5%)
  loops' own time  24 us (2%)
  other arithmetic  21.1 us (2%)
  between operations  13.8 us (1%)
    ppermute x3, waiting for transfers between devices, local(): lax.ppermute(left_gram, 'col', [(dev, dev ^ hop) for dev in range(8)])  276 us
    all_to_all x1, blocking collectives, local(): lax.all_to_all(gradient, 'col', split_axis=1, concat_axis=0, tiled=True)  213 us
    all_to_all x1, blocking collectives, local(): lax.all_to_all(tile_out, 'col', split_axis=0, concat_axis=1, tiled=True)  211 us
    psum x1, waiting for transfers between devices, local(): right_roots = lax.psum(jnp.stack(right_owned), 'row')  87.5 us
    psum x1, waiting for transfers between devices, local(): left_roots = lax.psum(jnp.stack(left_owned), 'col')  84.1 us
    dot_general x1, matrix products, local(): jnp.einsum('aibj,aibk->bjk', blocks, blocks, precision=lax.Precision.HIGH...  41 us
    dot_general x4, matrix products, product(): return jnp.matmul(first, second, precision=lax.Precision.HIGHEST)  32.4 us
    dot_general x1, matrix products, local(): jnp.einsum('aik,akbj->aibj', left_roots, blocks, precision=lax.Precision....  28.1 us
  transfers between devices with their start and end apart: 6, of which 5 were waited for; matrix products, arithmetic and copies ran while one was open for 11% of the time, Pallas kernels for 0%

profile of v1, /device:TPU:0, one launch (start us, length us, event | category | flops | bytes accessed | tf_op | source)
XLA Modules:
  0.0 1140.9 jit_solution(9208639304234540513)
XLA Ops:
  6.5 0.0 all-reduce.4.cloned.1.call-start
  6.5 4.5 copy.45
  11.1 212.6 %all_to_all.35 = f32[192,8,1536]{2,0,1:T(8,128)} all-to-all(f32[192,8,1536]{2,0,1:T(8,128)S(1)} %bitcast.97), channel_id=1, replica_groups=mesh['row'=4,'col'=8] {'col'}, dimensions={1} | all-to-all | bytes 18874368 | tf_op jit(solution)/shard_map/all_to_all | solution.py:35
  223.7 12.1 %reshape.108 = f32[2,768,2,768]{3,2,1,0:T(2,128)} reshape(f32[8,192,1536]{2,1,0:T(8,128)} %bitcast.95) | data formatting | bytes 18874368 | tf_op jit(solution)/shard_map/reshape | solution.py:38
  235.7 27.9 %bitcast_multiply_fusion = f32[2,768,768]{2,1,0:T(8,128)S(1)} fusion(f32[2,768,2,768]{3,2,1,0:T(2,128)} %reshape.108), kind=kOutput, calls=%fused_computation.132 | convolution fusion | flops 21744451584 | bytes 14155776 | tf_op jit(solution)/shard_map/aibj,akbj->aik/dot_general | solution.py:39
  263.6 0.1 collective-permute-start
  263.7 7.9 collective-permute-done
  271.6 0.0 slice-start
  271.6 0.0 slice-start.1
  271.6 0.6 add.63
  272.2 0.0 slice-start.2
  272.2 0.1 collective-permute-start.1
  272.3 103.8 %collective-permute-done.1 = f32[2,768,768]{2,1,0:T(8,128)S(1)} collective-permute-done((f32[2,768,768]{2,1,0:T(8,128)S(1)}, f32[2,768,768]{2,1,0:T(8,128)S(1)}, u32[]{:S(2)}, u32[]{:S(2)}) %collective-permute-start.1) | collective-permute-done | bytes 4718624 | tf_op jit(solution)/shard_map/ppermute | solution.py:43
  376.1 2.8 add.64
  378.9 0.1 collective-permute-start.2
  379.0 0.0 slice-done
  379.0 0.0 slice-done.1
  379.0 0.0 slice-done.2
  379.0 41.0 %bitcast_multiply_fusion.1 = f32[2,768,768]{2,1,0:T(8,128)} fusion(f32[2,768,2,768]{3,2,1,0:T(2,128)S(1)} %bitcast.99), kind=kOutput, calls=%fused_computation.133 | convolution fusion | flops 21744451584 | bytes 14155776 | tf_op jit(solution)/shard_map/aibj,aibk->bjk/dot_general | solution.py:40
  420.0 0.0 all-reduce.4.cloned.1.call-update
  420.0 0.0 all-reduce.8.cloned.1.call-start
  420.1 164.1 %collective-permute-done.2 = f32[2,768,768]{2,1,0:T(8,128)} collective-permute-done((f32[2,768,768]{2,1,0:T(8,128)}, f32[2,768,768]{2,1,0:T(8,128)}, u32[]{:S(2)}, u32[]{:S(2)}) %collective-permute-start.2) | collective-permute-done | bytes 4718624 | tf_op jit(solution)/shard_map/ppermute | solution.py:43
  584.2 6.6 add.65
  590.8 0.6 conditional.6
  590.8 0.2 stack.28
  591.4 14.2 %conditional.7 = (f32[1,768,768]{2,1,0:T(8,128)}) conditional(s32[]{:T(128)} %convert_element_type.19, () %tuple.40, f32[2,768,768]{2,1,0:T(8,128)} %add.65), branch_computations={%region_11.12_spmd, %region_12.0_spmd} | conditional | flops 21753888768 | bytes 40108140 | solution.py:57
  591.4 1.5 stack.30
  605.5 4.1 pad_maximum_fusion.1
  609.6 0.0 all-reduce.8.cloned.1.call-update
  609.7 0.0 all-reduce.6.cloned.1.call-start
  609.7 0.0 all-reduce.4.cloned.1.call-done
  609.8 10.1 conditional.5
  609.8 0.2 stack.26.clone
  619.8 39.5 %conditional.4 = (f32[1,768,768]{1,2,0:T(8,128)}) conditional(s32[]{:T(128)} %convert_element_type.16, () %tuple.37, f32[2,768,768]{2,1,0:T(8,128)} %all-reduce.4.cloned.1.call-done), branch_computations={%region_1.2_spmd, %region_2.4_spmd} | conditional | flops 21753888768 | bytes 49545304 | solution.py:65
  619.9 2.9 multiply_reduce_fusion
  623.5 8.6 fusion.5
  632.1 0.0 copy-start
  632.1 6.0 fusion.132
  638.1 0.0 copy-done
  638.1 7.5 fusion.7
  645.7 10.3 multiply_bitcast_fusion
  655.9 3.1 copy.29
  659.3 4.1 pad_maximum_fusion
  663.4 0.0 all-reduce.6.cloned.1.call-update
  663.4 84.1 %all-reduce.8.cloned.1.call-done = f32[2,768,768]{2,1,0:T(8,128)} async-done(((f32[2,768,768]{2,1,0:T(8,128)}), f32[2,768,768]{2,1,0:T(8,128)}) %all-reduce.8.cloned.1.call-update) | async-done | bytes 4718608 | tf_op jit(solution)/shard_map/psum | solution.py:67
  747.5 28.1 %fusion.118 = f32[2,768,2,768]{3,1,0,2:T(8,128)} fusion(f32[2,768,2,768]{3,2,1,0:T(2,128)} %reshape.108, f32[2,768,768]{2,1,0:T(8,128)} %all-reduce.8.cloned.1.call-done), kind=kOutput, calls=%fused_computation.123 | convolution fusion | flops 21743271936 | bytes 23592960 | tf_op jit(solution)/shard_map/aik,akbj->aibj/dot_general | solution.py:69
  775.6 87.5 %all-reduce.6.cloned.1.call-done = f32[2,768,768]{1,2,0:T(8,128)} async-done(((f32[2,768,768]{1,2,0:T(8,128)}), f32[2,768,768]{1,2,0:T(8,128)}) %all-reduce.6.cloned.1.call-update) | async-done | bytes 4718608 | tf_op jit(solution)/shard_map/psum | solution.py:68
  863.1 27.2 %fusion.125 = f32[2,768,2,768]{1,3,0,2:T(8,128)} fusion(f32[2,768,2,768]{3,1,0,2:T(8,128)} %fusion.118, f32[2,768,768]{1,2,0:T(8,128)} %all-reduce.6.cloned.1.call-done), kind=kOutput, calls=%fused_computation.134 | convolution fusion | flops 21743271936 | bytes 23592960 | tf_op jit(solution)/shard_map/aibj,bjl->aibl/dot_general | solution.py:70
  890.4 14.9 %copy.23 = f32[2,768,2,768]{3,2,1,0:T(2,128)} copy(f32[2,768,2,768]{1,3,0,2:T(8,128)} %fusion.125) | data formatting | bytes 18874368 | tf_op jit(solution)/shard_map/aibj,bjl->aibl/transpose | solution.py:70
  905.3 13.1 %all_to_all.29 = f32[8,192,1536]{2,1,0:T(8,128)} reshape(f32[2,768,2,768]{3,2,1,0:T(2,128)} %copy.23) | data formatting | bytes 18874368 | tf_op jit(solution)/shard_map/all_to_all | solution.py:72
  918.4 210.9 %all_to_all.36 = f32[8,192,1536]{2,1,0:T(8,128)S(1)} all-to-all(f32[8,192,1536]{2,1,0:T(8,128)} %all_to_all.29), channel_id=1, replica_groups=mesh['row'=4,'col'=8] {'col'}, dimensions={0} | all-to-all | bytes 18874368 | tf_op jit(solution)/shard_map/all_to_all | solution.py:72
  1129.3 4.6 copy.33
  (1 shorter events, 0.0 us)
Async XLA Ops:
  6.5 603.2 %all-reduce.4.cloned.1.call-start = ((), (), s32[]{:S(2)}) async-start(), calls=%async_computation.2 | async-start | bytes 9437184 | tf_op jit(solution)/shard_map/psum | solution.py:46
  263.6 8.0 collective-permute-start
  271.6 107.5 %slice-start = ((s8[9437184]{0:T(1024)(128)(4,1)}), s8[4194304]{0:T(1024)(128)(4,1)S(1)}, s32[]{:S(2)}) async-start(s8[9437184]{0:T(1024)(128)(4,1)} %bitcast.98), calls=%async_computation.5 | async-start | bytes 8388608
  271.6 107.5 %slice-start.1 = ((s8[9437184]{0:T(1024)(128)(4,1)}), s8[4194304]{0:T(1024)(128)(4,1)S(1)}, s32[]{:S(2)}) async-start(s8[9437184]{0:T(1024)(128)(4,1)} %bitcast.98), calls=%async_computation.6 | async-start | bytes 8388608
  272.2 106.8 %slice-start.2 = ((s8[9437184]{0:T(1024)(128)(4,1)}), s8[1048576]{0:T(1024)(128)(4,1)S(1)}, s32[]{:S(2)}) async-start(s8[9437184]{0:T(1024)(128)(4,1)} %bitcast.98), calls=%async_computation.7 | async-start | bytes 2097152
  272.2 103.9 %collective-permute-start.1 = (f32[2,768,768]{2,1,0:T(8,128)S(1)}, f32[2,768,768]{2,1,0:T(8,128)S(1)}, u32[]{:S(2)}, u32[]{:S(2)}) collective-permute-start(f32[2,768,768]{2,1,0:T(8,128)S(1)} %add.63), channel_id=1, source_target_pairs={{0,2},{1,3},{2,0},{3,1},{4,6},{5,7},{6,4},{7,5},{8,10},{9,11},{10,... | collective-permute-start | bytes 14155784 | tf_op jit(solution)/shard_map/ppermute | solution.py:43
  378.9 205.3 %collective-permute-start.2 = (f32[2,768,768]{2,1,0:T(8,128)}, f32[2,768,768]{2,1,0:T(8,128)}, u32[]{:S(2)}, u32[]{:S(2)}) collective-permute-start(f32[2,768,768]{2,1,0:T(8,128)} %add.64), channel_id=1, source_target_pairs={{0,4},{1,5},{2,6},{3,7},{4,0},{5,1},{6,2},{7,3},{8,12},{9,13},{10,... | collective-permute-start | bytes 14155784 | tf_op jit(solution)/shard_map/ppermute | solution.py:43
  420.0 327.5 %all-reduce.8.cloned.1.call-start = ((), (), s32[]{:S(2)}) async-start(), calls=%async_computation.4 | async-start | bytes 9437184 | tf_op jit(solution)/shard_map/psum | solution.py:67
  609.7 253.5 %all-reduce.6.cloned.1.call-start = ((), (), s32[]{:S(2)}) async-start(), calls=%async_computation.3 | async-start | bytes 9437184 | tf_op jit(solution)/shard_map/psum | solution.py:68
  632.1 6.0 copy-start
Sparse Core Ops, SparseCore 0:
  420.1 112.7 all-reduce.3
  609.8 137.6 all-reduce.7
  750.8 112.3 all-reduce.5
